TPU v7x, 256 devices: a whole 4x4x8 slice. The times are simulated.
256 devices in a mesh: row: 8 (over z), col: 32 (over y, x, core).
Axes of the slice: x: 4, y: 4, z: 8, core: 2. Of those that a mesh axis runs over, the one named last changes fastest.
Arguments:
- matrix: float32 [16384, 16384], P('row', 'col'), may hold values from -48 to 48, as said below
- pivots: int32 [2, 64], replicated, may hold values from 128 to 16383, as said below
Outputs:
- factored: float32 [16384, 16384], P('row', 'col')
Inputs may be any that keep to these rules, and one draw needn't show every extreme that they name: `pivots`: the 128 entries are distinct global row numbers. `matrix`: the entry of row pivots[c, k] in global column c * 64 + k dominates the other entries of its global column, so that multipliers stay well below one.
All inputs are finite; a program needn't handle non-finite values.
Results may differ from a plain program's by a relative error of at most 0.0002.
Values sent between devices are 32-bit elements; how exact they have to be, the bound alone decides.
A program may use at most 64 MiB of HBM per device.

v0:
```python
import jax
import jax.numpy as jnp
from jax import lax
from jax.experimental import pallas as pl
from jax.experimental.pallas import tpu as pltpu
from jax.sharding import PartitionSpec as P

NB = 64
TOP = 2 * NB
SUB = 8
CHUNKS = 8
PLACES = 8
HIGHEST = lax.Precision.HIGHEST
MESH = pl.DeviceIdType.MESH


def dot(a, b):
    return lax.dot_general(
        a, b, (((1,), (0,)), ((), ())), precision=HIGHEST, preferred_element_type=jnp.float32
    )


def place_of(pivot_ref, k):
    grid_rows = lax.axis_size("row")
    bits = NB.bit_length() - 1
    pivot = pivot_ref[k >> bits, k & (NB - 1)]
    local = (pivot >> (bits + grid_rows.bit_length() - 1) << bits) + (pivot & (NB - 1))
    mine = (pivot >> bits & (grid_rows - 1)) == lax.axis_index("row")
    return jnp.where(mine, local, -1)


def halves(x):
    high = x.astype(jnp.bfloat16)
    return high, (x - high.astype(jnp.float32)).astype(jnp.bfloat16)


def dot_pair(a, b):
    return lax.dot_general(
        a, b, (((1,), (0,)), ((), ())), preferred_element_type=jnp.float32
    )


def spread(block, lane):
    return jnp.broadcast_to(block[:, lane : lane + 1], block.shape)


def line(block, row):
    return jnp.broadcast_to(block[row : row + 1, :], block.shape)


def factor(a_ref, lu_ref, linv_ref, uinv_ref):
    n = TOP // SUB
    lane = lax.broadcasted_iota(jnp.int32, (SUB, TOP), 1)
    sub = lax.broadcasted_iota(jnp.int32, (SUB, TOP), 0)
    a = [a_ref[SUB * i : SUB * (i + 1), :] for i in range(n)]
    low = [jnp.where(lane == sub + SUB * i, 1.0, 0.0).astype(jnp.float32) for i in range(n)]
    upp = list(low)
    weights = jnp.ones((SUB, TOP), jnp.float32)
    for b in range(n):
        first = SUB * b
        cols = [spread(a[b], first + j) for j in range(SUB)]
        weight, entry, a_line, low_line = [], [], [], []
        for k in range(SUB):
            weight.append(1.0 / line(cols[k], k))
            weights = jnp.where(lane == first + k, weight[k], weights)
            entry.append([line(cols[j], k) if j > k else None for j in range(SUB)])
            a_line.append(jnp.where(lane > first + k, line(a[b], k), 0.0))
            low_line.append(line(low[b], k))
            if k < SUB - 1:
                multiplier = jnp.where(sub > k, cols[k] * weight[k], 0.0)
                for j in range(k + 1, SUB):
                    cols[j] = cols[j] - multiplier * entry[k][j]
                a[b] = a[b] - multiplier * a_line[k]
                low[b] = low[b] - multiplier * low_line[k]

        def multipliers(cols):
            cols = list(cols)
            for k in range(SUB):
                cols[k] = cols[k] * weight[k]
                for j in range(k + 1, SUB):
                    cols[j] = cols[j] - cols[k] * entry[k][j]
            return cols

        for i in range(b + 1, n):
            part = multipliers([spread(a[i], first + j) for j in range(SUB)])
            for k in range(SUB):
                a[i] = a[i] - part[k] * a_line[k]
                low[i] = low[i] - part[k] * low_line[k]
        for i in range(b + 1):
            if i == b:
                part = [jnp.where(sub == j, 1.0, 0.0).astype(jnp.float32) for j in range(SUB)]
            else:
                part = [spread(upp[i], first + j) for j in range(SUB)]
            part = multipliers(part)
            for k in range(SUB):
                upp[i] = upp[i] - part[k] * a_line[k]
    for i in range(n):
        part = slice(SUB * i, SUB * (i + 1))
        lu_ref[part, :] = jnp.where(sub + SUB * i > lane, a[i] * weights, a[i])
        linv_ref[part, :] = low[i]
        uinv_ref[part, :] = upp[i] * weights


def finish_kernel(
    pivot_ref,
    a_ref,
    panel_ref,
    lead_ref,
    new_top_ref,
    old_top_ref,
    old_lead_ref,
    out_ref,
    a_buf,
    p_buf,
    lu,
    linv,
    uinv,
    upper,
    solved,
    top_rows,
    in_sem,
    panel_sem,
    out_sem,
):
    my_row = lax.axis_index("row")
    my_col = lax.axis_index("col")
    rows = a_buf.shape[0] // CHUNKS
    copies = [
        pltpu.make_async_copy(
            a_ref.at[pl.ds(rows * i, rows)], a_buf.at[pl.ds(rows * i, rows)], in_sem.at[i]
        )
        for i in range(CHUNKS)
    ]
    panel_copy = pltpu.make_async_copy(panel_ref, p_buf, panel_sem)
    panel_copy.start()
    for copy in copies:
        copy.start()
    factor(lead_ref, lu, linv, uinv)
    upper[...] = dot(linv[...], new_top_ref[...])
    solved[...] = dot(uinv[...], upper[...])
    holds = my_col < 2
    own_lanes = (lax.broadcasted_iota(jnp.int32, (TOP, TOP), 1) < NB) & holds
    inverse = uinv[...]
    own = jnp.where(my_col == 0, inverse, pltpu.roll(inverse, NB, 1))
    solved[:, :TOP] = jnp.where(own_lanes, -own, solved[:, :TOP])
    top = pl.ds(pl.multiple_of(jnp.minimum(my_row, 1) * NB, NB), NB)
    corner = lu[top, :]
    corner = jnp.where(my_col == 0, corner, pltpu.roll(corner, NB, 1))
    top_rows[...] = upper[top, :]
    top_rows[:, :TOP] = jnp.where(own_lanes[:NB], corner, top_rows[:, :TOP])
    high, rest = halves(solved[...])
    twice = jnp.concatenate([high, high], axis=0)
    panel_copy.wait()
    for copy in copies:
        copy.wait()

    def place(step, carry):
        for j in range(PLACES):
            k = step * PLACES + j
            index = place_of(pivot_ref, k)

            @pl.when(index >= 0)
            def _():
                a_buf[pl.ds(index, 1), :] = old_top_ref[pl.ds(k, 1), :]
                p_buf[pl.ds(index, 1), :] = old_lead_ref[pl.ds(k, 1), :]

        return carry

    lax.fori_loop(0, TOP // PLACES, place, 0)
    dropped = (lax.broadcasted_iota(jnp.int32, (rows, a_buf.shape[1]), 1) < NB) & holds
    outs = []
    for i in range(CHUNKS):
        part = pl.ds(rows * i, rows)
        kept = jnp.where(dropped, 0.0, a_buf[part, :])
        left, left_rest = halves(p_buf[part, :])
        product = dot_pair(jnp.concatenate([left, left_rest], axis=1), twice)
        a_buf[part, :] = kept - (product + dot_pair(left, rest))
        if i == 0:

            @pl.when(my_row < 2)
            def _():
                a_buf[:NB, :] = top_rows[...]

        out = pltpu.make_async_copy(a_buf.at[part], out_ref.at[part], out_sem.at[i])
        out.start()
        outs.append(out)
    for out in outs:
        out.wait()


def finish(matrix, panel, lead, new_top, old_top, old_lead, pivots):
    any_spec = pl.BlockSpec(memory_space=pl.ANY)
    vmem = pl.BlockSpec(memory_space=pltpu.VMEM)
    return pl.pallas_call(
        finish_kernel,
        out_shape=jax.ShapeDtypeStruct(matrix.shape, jnp.float32),
        in_specs=[pl.BlockSpec(memory_space=pltpu.SMEM), any_spec, any_spec] + [vmem] * 4,
        out_specs=any_spec,
        scratch_shapes=[
            pltpu.VMEM(matrix.shape, jnp.float32),
            pltpu.VMEM(panel.shape, jnp.float32),
            pltpu.VMEM((TOP, TOP), jnp.float32),
            pltpu.VMEM((TOP, TOP), jnp.float32),
            pltpu.VMEM((TOP, TOP), jnp.float32),
            pltpu.VMEM(new_top.shape, jnp.float32),
            pltpu.VMEM(new_top.shape, jnp.float32),
            pltpu.VMEM((NB, new_top.shape[1]), jnp.float32),
            pltpu.SemaphoreType.DMA((CHUNKS,)),
            pltpu.SemaphoreType.DMA,
            pltpu.SemaphoreType.DMA((CHUNKS,)),
        ],
        name="finish",
    )(pivots, matrix, panel, lead, new_top, old_top, old_lead)


def move_kernel(
    pivot_ref,
    a_ref,
    panel_ref,
    new_ref,
    old_ref,
    lead_ref,
    old_lead_ref,
    a_buf,
    lead_buf,
    picked_lead,
    pack,
    picked,
    parts,
    news,
    olds,
    tiles,
    tile_parts,
    tile_pair,
    leads,
    load_sem,
    slice_send,
    slice_recv,
    spread_send,
    pair_send,
    pair_recv,
    part_send,
    part_recv,
    top_send,
    top_recv,
    new_send,
    new_recv,
    old_send,
    old_recv,
    tile_send,
    tile_recv,
    fan_send,
    fan_recv,
    lead_send,
    lead_recv,
):
    rows_dev = lax.axis_size("row")
    cols_dev = lax.axis_size("col")
    chips = cols_dev // 2
    my_row = lax.axis_index("row")
    my_col = lax.axis_index("col")
    chip = my_col // 2
    core = my_col % 2
    chunk = TOP // rows_dev
    half_rows = a_buf.shape[0] // 2
    slice_rows = half_rows // chips

    load_lead = pltpu.make_async_copy(a_ref.at[:, pl.ds(0, TOP)], lead_buf, load_sem.at[0])
    load = pltpu.make_async_copy(a_ref, a_buf, load_sem.at[1])

    @pl.when(chip == 0)
    def _():
        load_lead.start()

    load.start()
    barrier = pltpu.get_barrier_semaphore()
    for j in range(1, rows_dev):
        pl.semaphore_signal(
            barrier, inc=1, device_id={"row": lax.rem(my_row + j, rows_dev)}, device_id_type=MESH
        )
    for j in range(1, cols_dev):
        pl.semaphore_signal(
            barrier, inc=1, device_id={"col": lax.rem(my_col + j, cols_dev)}, device_id_type=MESH
        )

    def pick(table, target):
        def body(step, carry):
            for j in range(PLACES):
                k = step * PLACES + j
                index = place_of(pivot_ref, k)
                row = table[pl.ds(jnp.maximum(index, 0), 1), :]
                target[pl.ds(k, 1), :] = jnp.where(index >= 0, row, 0.0)
            return carry

        lax.fori_loop(0, TOP // PLACES, body, 0)

    first = lax.broadcasted_iota(jnp.int32, (slice_rows, TOP), 1) < NB
    first_tile = lax.broadcasted_iota(jnp.int32, (chunk, TOP), 1) < NB

    def top_start(d):
        return d * chunk - d * chunk // NB * NB

    @pl.when(chip == 0)
    def _():
        load_lead.wait()
        pick(lead_buf, picked_lead)
        for d in range(rows_dev):
            start = top_start(d)
            top = pltpu.roll(lead_buf[start : start + chunk, :], NB, 1)
            top = jnp.where(my_row == d * chunk // NB, top, 0.0)
            tiles[d] = jnp.where(first_tile, picked_lead[chunk * d : chunk * (d + 1), :], top)

    @pl.when(chip != 0)
    def _():
        load.wait()
        pick(a_buf, picked)

    pl.semaphore_wait(barrier, rows_dev + cols_dev - 2)

    def to_row(source, target, send, recv, d):
        return pltpu.make_async_remote_copy(
            src_ref=source,
            dst_ref=target,
            send_sem=send,
            recv_sem=recv,
            device_id={"row": d},
            device_id_type=MESH,
        )

    def to_col(source, target, send, recv, q):
        return pltpu.make_async_remote_copy(
            src_ref=source,
            dst_ref=target,
            send_sem=send,
            recv_sem=recv,
            device_id={"col": q},
            device_id_type=MESH,
        )

    def other(j):
        return lax.rem(my_row + j, rows_dev)

    def tile_copy(j):
        d = other(j)
        return to_row(
            tiles.at[d], tile_parts.at[my_row], tile_send.at[j], tile_recv.at[my_row], d
        )

    def slice_copy(s, t, send):
        return to_col(pack.at[core, s], pack.at[core, s], send, slice_recv.at[s], t * 2 + core)

    def part_copy(j):
        d = other(j)
        return to_row(
            picked.at[pl.ds(d * chunk, chunk)],
            parts.at[my_row],
            part_send.at[j],
            part_recv.at[my_row],
            d,
        )

    def top_copy(d):
        return to_row(
            a_buf.at[pl.ds(top_start(d), chunk), :], olds.at[d], top_send.at[d], top_recv, d
        )

    def ring_copy(j, table, send, recv):
        return to_row(table.at[my_row], table.at[my_row], send.at[j], recv.at[my_row], other(j))

    def arrive(j, table, send, recv):
        s = other(j)
        to_row(table.at[s], table.at[s], send.at[j], recv.at[s], s).wait_recv()

    two_stage = rows_dev == 8

    def hop(table, slot, part, d, send, recv):
        return to_row(table.at[slot, part], table.at[slot, part], send, recv, d)

    def stage_one(table, send, recv):
        return [
            hop(table, my_row, pl.ds(0, chunk), other(j), send.at[j], recv.at[my_row])
            for j in ((2, 6) if two_stage else range(1, rows_dev))
        ]

    def stage_two(table, send, recv):
        if not two_stage:
            return []
        whole = pl.ds(0, chunk)
        below, above = other(6), other(2)
        return [
            hop(table, below, whole, other(7), send.at[0], recv.at[below]),
            hop(table, below, whole, other(1), send.at[1], recv.at[below]),
            hop(table, below, pl.ds(0, chunk // 2), other(2), send.at[3], recv.at[below]),
            hop(table, above, whole, other(1), send.at[4], recv.at[above]),
            hop(table, above, whole, other(7), send.at[5], recv.at[above]),
            hop(
                table,
                above,
                pl.ds(chunk // 2, chunk // 2),
                other(6),
                send.at[7],
                recv.at[rows_dev],
            ),
        ]

    def begin(table, send, recv):
        for copy in stage_one(table, send, recv):
            copy.start()

    def forward(table, send, recv):
        if two_stage:
            arrive(6, table, send, recv)
            arrive(2, table, send, recv)
        for copy in stage_two(table, send, recv):
            copy.start()

    def gathered(table, send, recv):
        if not two_stage:
            for j in range(1, rows_dev):
                arrive(j, table, send, recv)
            return
        for j in (1, 3, 5, 7):
            arrive(j, table, send, recv)
        far = other(4)
        half = chunk // 2
        hop(table, far, pl.ds(0, half), far, send.at[0], recv.at[far]).wait_recv()
        hop(table, far, pl.ds(half, half), far, send.at[0], recv.at[rows_dev]).wait_recv()

    def sent(table, send, recv):
        for copy in stage_one(table, send, recv) + stage_two(table, send, recv):
            copy.wait_send()

    def fan_copy(j):
        q = lax.rem(my_col + j, cols_dev)
        return to_col(
            tile_pair.at[core], tile_pair.at[core], fan_send.at[j], fan_recv.at[core], q
        )

    @pl.when(chip == 0)
    def _():
        for j in range(1, rows_dev):
            tile_copy(j).start()
        tile_parts[my_row] = tiles[my_row]
        for s in range(chips):
            low = lead_buf[slice_rows * s : slice_rows * (s + 1), :]
            high = lead_buf[half_rows + slice_rows * s : half_rows + slice_rows * (s + 1), :]
            at_zero = jnp.where(core == 0, low, high)
            shifted = jnp.where(core == 0, high, low)
            pack[core, s] = jnp.where(first, at_zero, pltpu.roll(shifted, NB, 1))
        for s in range(1, chips):
            slice_copy(s, s, slice_send.at[s]).start()
        load.wait()
        pick(a_buf, picked)

    for j in range(1, rows_dev):
        part_copy(j).start()
    parts[my_row] = picked[pl.ds(pl.multiple_of(my_row * chunk, chunk), chunk), :]
    for d in range(rows_dev):
        owner = d * chunk // NB

        @pl.when(my_row == owner)
        def _():
            if d == owner:
                olds[d] = a_buf[top_start(d) : top_start(d) + chunk, :]
            else:
                top_copy(d).start()

    @pl.when(chip == 0)
    def _():
        for j in range(1, rows_dev):
            arrive(j, tile_parts, tile_send, tile_recv)
        total = tile_parts[0]
        for s in range(1, rows_dev):
            total = total + tile_parts[s]
        tile_pair[core] = total
        for j in range(1, cols_dev):
            fan_copy(j).start()

    @pl.when(chip != 0)
    def _():
        slice_copy(chip, chip, slice_send.at[0]).wait_recv()

    for j in range(1, chips):
        t = lax.rem(chip + j, chips)

        @pl.when(t != 0)
        def _():
            slice_copy(chip, t, spread_send.at[j]).start()

    for d in range(rows_dev):
        if d != d * chunk // NB:

            @pl.when(my_row == d)
            def _():
                top_copy(d).wait_recv()

    begin(olds, old_send, old_recv)
    for j in range(1, rows_dev):
        arrive(j, parts, part_send, part_recv)
    total = parts[0]
    for s in range(1, rows_dev):
        total = total + parts[s]
    news[my_row] = total
    begin(news, new_send, new_recv)
    forward(olds, old_send, old_recv)

    for c in range(2):

        @pl.when(my_col != c)
        def _():
            to_col(
                tile_pair.at[c], tile_pair.at[c], fan_send.at[0], fan_recv.at[c], c
            ).wait_recv()

    zero_tile = tile_pair[0]
    one_tile = tile_pair[1]
    leads[my_row, :chunk] = jnp.where(first_tile, zero_tile, pltpu.roll(one_tile, NB, 1))
    leads[my_row, chunk:] = jnp.where(first_tile, pltpu.roll(zero_tile, NB, 1), one_tile)
    for j in range(1, rows_dev):
        ring_copy(j, leads, lead_send, lead_recv).start()
    forward(news, new_send, new_recv)

    groups = min(4, chips)
    per = chips // groups

    def pair_copy(g, which):
        held = pack.at[which, pl.ds(g * per, per)]
        return to_col(held, held, pair_send.at[g], pair_recv.at[g], chip * 2 + 1 - core)

    for g in range(groups):

        @pl.when(chip != 0)
        def _():
            for s in range(g * per, (g + 1) * per):

                @pl.when(chip != s)
                def _():
                    slice_copy(s, chip, slice_send.at[0]).wait_recv()

        pair_copy(g, core).start()

    for g in range(groups):
        pair_copy(g, 1 - core).wait_recv()
        for s in range(g * per, (g + 1) * per):
            zero_pack = pack[0, s]
            one_pack = pack[1, s]
            low = slice(slice_rows * s, slice_rows * (s + 1))
            high = slice(half_rows + slice_rows * s, half_rows + slice_rows * (s + 1))
            panel_ref[low, :] = jnp.where(first, zero_pack, one_pack)
            panel_ref[high, :] = pltpu.roll(jnp.where(first, one_pack, zero_pack), NB, 1)

    for j in range(1, rows_dev):
        arrive(j, leads, lead_send, lead_recv)
    gathered(news, new_send, new_recv)
    for d in range(rows_dev):
        part = slice(chunk * d, chunk * (d + 1))
        lead_ref[part, :] = leads[d, :chunk]
        old_lead_ref[part, :] = leads[d, chunk:]
        new_ref[part, :] = news[d]
    gathered(olds, old_send, old_recv)
    for d in range(rows_dev):
        old_ref[chunk * d : chunk * (d + 1), :] = olds[d]

    for j in range(1, rows_dev):
        part_copy(j).wait_send()
        ring_copy(j, leads, lead_send, lead_recv).wait_send()
    sent(news, new_send, new_recv)
    sent(olds, old_send, old_recv)
    for d in range(rows_dev):
        owner = d * chunk // NB
        if d != owner:

            @pl.when(my_row == owner)
            def _():
                top_copy(d).wait_send()

    @pl.when(chip == 0)
    def _():
        for j in range(1, rows_dev):
            tile_copy(j).wait_send()
        for s in range(1, chips):
            slice_copy(s, s, slice_send.at[s]).wait_send()
        for j in range(1, cols_dev):
            fan_copy(j).wait_send()

    for j in range(1, chips):
        t = lax.rem(chip + j, chips)

        @pl.when(t != 0)
        def _():
            slice_copy(chip, t, spread_send.at[j]).wait_send()

    for g in range(groups):
        pair_copy(g, core).wait_send()


def move(matrix, pivots):
    rows_dev = lax.axis_size("row")
    cols_dev = lax.axis_size("col")
    chips = cols_dev // 2
    chunk = TOP // rows_dev
    rows, cols = matrix.shape
    dma = pltpu.SemaphoreType.DMA
    f32 = jnp.float32
    vmem = pl.BlockSpec(memory_space=pltpu.VMEM)
    by_row = dma((rows_dev,))
    by_chip = dma((chips,))
    return pl.pallas_call(
        move_kernel,
        out_shape=[
            jax.ShapeDtypeStruct((rows, TOP), f32),
            jax.ShapeDtypeStruct((TOP, cols), f32),
            jax.ShapeDtypeStruct((TOP, cols), f32),
            jax.ShapeDtypeStruct((TOP, TOP), f32),
            jax.ShapeDtypeStruct((TOP, TOP), f32),
        ],
        in_specs=[
            pl.BlockSpec(memory_space=pltpu.SMEM),
            pl.BlockSpec(memory_space=pl.ANY),
        ],
        out_specs=[vmem] * 5,
        scratch_shapes=[
            pltpu.VMEM((rows, cols), f32),
            pltpu.VMEM((rows, TOP), f32),
            pltpu.VMEM((TOP, TOP), f32),
            pltpu.VMEM((2, chips, rows // 2 // chips, TOP), f32),
            pltpu.VMEM((TOP, cols), f32),
            pltpu.VMEM((rows_dev, chunk, cols), f32),
            pltpu.VMEM((rows_dev, chunk, cols), f32),
            pltpu.VMEM((rows_dev, chunk, cols), f32),
            pltpu.VMEM((rows_dev, chunk, TOP), f32),
            pltpu.VMEM((rows_dev, chunk, TOP), f32),
            pltpu.VMEM((2, chunk, TOP), f32),
            pltpu.VMEM((rows_dev, 2 * chunk, TOP), f32),
            dma((2,)),
            by_chip,
            by_chip,
            by_chip,
            dma((4,)),
            dma((4,)),
            by_row,
            by_row,
            by_row,
            dma,
            by_row,
            dma((rows_dev + 1,)),
            by_row,
            dma((rows_dev + 1,)),
            by_row,
            by_row,
            dma((cols_dev,)),
            dma((2,)),
            by_row,
            by_row,
        ],
        compiler_params=pltpu.CompilerParams(collective_id=0, has_side_effects=True),
        name="move",
    )(pivots, matrix)


def shards(matrix, pivots):
    panel, new_top, old_top, lead, old_lead = move(matrix, pivots)
    return finish(matrix, panel, lead, new_top, old_top, old_lead, pivots)


def solution(mesh):
    placed = (P("row", "col"), P())
    return jax.shard_map(
        shards, mesh=mesh, in_specs=placed, out_specs=P("row", "col"), check_vma=False
    )
```

profile of v0, /device:TPU:32, one launch (start us, length us, event | category | flops | bytes accessed | tf_op | source)
XLA Modules:
  0.0 47.0 jit_solution(15993535519131804871)
XLA Ops:
  0.0 34.8 %move.1 = (f32[2048,128]{1,0:T(8,128)}, f32[128,512]{1,0:T(8,128)}, f32[128,512]{1,0:T(8,128)}, f32[128,128]{1,0:T(8,128)}, f32[128,128]{1,0:T(8,128)}) custom-call(s32[2,64]{1,0:T(2,128)} %pivot_ref.3, f32[2048,512]{1,0:T(8,128)} %a_ref.3), custom_call_target="tpu_custom_call" | custom-call | tf_op jit(solution)/shard_map/move/pallas_call | solution.py:608
  34.8 12.1 %finish.1 = f32[2048,512]{1,0:T(8,128)} custom-call(s32[2,64]{1,0:T(2,128)} %pivot_ref.3, f32[2048,512]{1,0:T(8,128)} %a_ref.3, f32[2048,128]{1,0:T(8,128)} %get-tuple-element.10.panel_ref, f32[128,128]{1,0:T(8,128)} %get-tuple-element.11.lead_ref, f32[128,512]{1,0:T(8,128)} %get-tuple-element.12.new_top_ref, f32[128,512]{1,0:T(8,128)} %get-tuple-element.13.old_top_ref, ...), custom_call_target="tpu_custom_call" | custom-call | tf_op jit(solution)/shard_map/finish/pallas_call | solution.py:194
where the time goes:
time: 47.2 us; the launch traced here: 47 us
  Pallas kernels  47 us (100%)
    pallas_call x1, Pallas kernels, move(): pl.pallas_call(move_kernel, out_shape=[jax.ShapeDtypeStruct((rows, TOP),...  34.8 us
    pallas_call x1, Pallas kernels, finish(): pl.pallas_call(finish_kernel, out_shape=jax.ShapeDtypeStruct(matrix.shape...  12.1 us

commit v1 on v0

--- a/solution.py
+++ b/solution.py
@@ -10,14 +10,7 @@
 SUB = 8
 CHUNKS = 8
 PLACES = 8
-HIGHEST = lax.Precision.HIGHEST
 MESH = pl.DeviceIdType.MESH
-
-
-def dot(a, b):
-    return lax.dot_general(
-        a, b, (((1,), (0,)), ((), ())), precision=HIGHEST, preferred_element_type=jnp.float32
-    )
 
 
 def place_of(pivot_ref, k):
@@ -40,6 +33,13 @@
     )
 
 
+def dot(a, b):
+    high, rest = halves(a)
+    b_high, b_rest = halves(b)
+    both = jnp.concatenate([high, rest], axis=1)
+    return dot_pair(both, jnp.concatenate([b_high, b_high], axis=0)) + dot_pair(high, b_rest)
+
+
 def spread(block, lane):
     return jnp.broadcast_to(block[:, lane : lane + 1], block.shape)
 
@@ -52,7 +52,11 @@
     n = TOP // SUB
     lane = lax.broadcasted_iota(jnp.int32, (SUB, TOP), 1)
     sub = lax.broadcasted_iota(jnp.int32, (SUB, TOP), 0)
-    a = [a_ref[SUB * i : SUB * (i + 1), :] for i in range(n)]
+    chunk = a_ref.shape[1] // 2
+    a = []
+    for i in range(n):
+        slot, start = divmod(SUB * i, chunk)
+        a.append(a_ref[slot, start : start + SUB, :])
     low = [jnp.where(lane == sub + SUB * i, 1.0, 0.0).astype(jnp.float32) for i in range(n)]
     upp = list(low)
     weights = jnp.ones((SUB, TOP), jnp.float32)
@@ -105,13 +109,14 @@
     pivot_ref,
     a_ref,
     panel_ref,
-    lead_ref,
-    new_top_ref,
-    old_top_ref,
-    old_lead_ref,
+    leads_ref,
+    news_ref,
+    olds_ref,
     out_ref,
     a_buf,
     p_buf,
+    news,
+    olds,
     lu,
     linv,
     uinv,
@@ -119,7 +124,7 @@
     solved,
     top_rows,
     in_sem,
-    panel_sem,
+    side_sem,
     out_sem,
 ):
     my_row = lax.axis_index("row")
@@ -131,12 +136,16 @@
         )
         for i in range(CHUNKS)
     ]
-    panel_copy = pltpu.make_async_copy(panel_ref, p_buf, panel_sem)
-    panel_copy.start()
+    news_copy = pltpu.make_async_copy(news_ref, news, side_sem.at[0])
+    olds_copy = pltpu.make_async_copy(olds_ref, olds, side_sem.at[1])
+    panel_copy = pltpu.make_async_copy(panel_ref, p_buf, side_sem.at[2])
+    for copy in (news_copy, olds_copy, panel_copy):
+        copy.start()
     for copy in copies:
         copy.start()
-    factor(lead_ref, lu, linv, uinv)
-    upper[...] = dot(linv[...], new_top_ref[...])
+    factor(leads_ref, lu, linv, uinv)
+    news_copy.wait()
+    upper[...] = dot(linv[...], news[...].reshape(upper.shape))
     solved[...] = dot(uinv[...], upper[...])
     holds = my_col < 2
     own_lanes = (lax.broadcasted_iota(jnp.int32, (TOP, TOP), 1) < NB) & holds
@@ -150,9 +159,13 @@
     top_rows[:, :TOP] = jnp.where(own_lanes[:NB], corner, top_rows[:, :TOP])
     high, rest = halves(solved[...])
     twice = jnp.concatenate([high, high], axis=0)
+    olds_copy.wait()
     panel_copy.wait()
     for copy in copies:
         copy.wait()
+
+    chunk = olds.shape[1]
+    bits = chunk.bit_length() - 1
 
     def place(step, carry):
         for j in range(PLACES):
@@ -161,8 +174,10 @@
 
             @pl.when(index >= 0)
             def _():
-                a_buf[pl.ds(index, 1), :] = old_top_ref[pl.ds(k, 1), :]
-                p_buf[pl.ds(index, 1), :] = old_lead_ref[pl.ds(k, 1), :]
+                slot = k >> bits
+                row = k & (chunk - 1)
+                a_buf[pl.ds(index, 1), :] = olds[slot, pl.ds(row, 1), :]
+                p_buf[pl.ds(index, 1), :] = leads_ref[slot, pl.ds(chunk + row, 1), :]
 
         return carry
 
@@ -188,39 +203,40 @@
         out.wait()
 
 
-def finish(matrix, panel, lead, new_top, old_top, old_lead, pivots):
+def finish(matrix, panel, leads, news, olds, pivots):
     any_spec = pl.BlockSpec(memory_space=pl.ANY)
     vmem = pl.BlockSpec(memory_space=pltpu.VMEM)
     return pl.pallas_call(
         finish_kernel,
         out_shape=jax.ShapeDtypeStruct(matrix.shape, jnp.float32),
-        in_specs=[pl.BlockSpec(memory_space=pltpu.SMEM), any_spec, any_spec] + [vmem] * 4,
+        in_specs=[pl.BlockSpec(memory_space=pltpu.SMEM), any_spec, any_spec, vmem, any_spec, any_spec],
         out_specs=any_spec,
         scratch_shapes=[
             pltpu.VMEM(matrix.shape, jnp.float32),
             pltpu.VMEM(panel.shape, jnp.float32),
+            pltpu.VMEM(news.shape, jnp.float32),
+            pltpu.VMEM(olds.shape, jnp.float32),
             pltpu.VMEM((TOP, TOP), jnp.float32),
             pltpu.VMEM((TOP, TOP), jnp.float32),
             pltpu.VMEM((TOP, TOP), jnp.float32),
-            pltpu.VMEM(new_top.shape, jnp.float32),
-            pltpu.VMEM(new_top.shape, jnp.float32),
-            pltpu.VMEM((NB, new_top.shape[1]), jnp.float32),
+            pltpu.VMEM((TOP, matrix.shape[1]), jnp.float32),
+            pltpu.VMEM((TOP, matrix.shape[1]), jnp.float32),
+            pltpu.VMEM((NB, matrix.shape[1]), jnp.float32),
             pltpu.SemaphoreType.DMA((CHUNKS,)),
-            pltpu.SemaphoreType.DMA,
+            pltpu.SemaphoreType.DMA((3,)),
             pltpu.SemaphoreType.DMA((CHUNKS,)),
         ],
         name="finish",
-    )(pivots, matrix, panel, lead, new_top, old_top, old_lead)
+    )(pivots, matrix, panel, leads, news, olds)
 
 
 def move_kernel(
     pivot_ref,
     a_ref,
     panel_ref,
-    new_ref,
-    old_ref,
-    lead_ref,
-    old_lead_ref,
+    leads_ref,
+    news_ref,
+    olds_ref,
     a_buf,
     lead_buf,
     picked_lead,
@@ -233,6 +249,8 @@
     tile_parts,
     tile_pair,
     leads,
+    sums,
+    panel,
     load_sem,
     slice_send,
     slice_recv,
@@ -253,6 +271,8 @@
     fan_recv,
     lead_send,
     lead_recv,
+    panel_out,
+    side_out,
 ):
     rows_dev = lax.axis_size("row")
     cols_dev = lax.axis_size("col")
@@ -349,15 +369,41 @@
     def slice_copy(s, t, send):
         return to_col(pack.at[core, s], pack.at[core, s], send, slice_recv.at[s], t * 2 + core)
 
-    def part_copy(j):
-        d = other(j)
+    half = chunk // 2
+    all_rows = pl.ds(0, chunk)
+
+    def part_of(d, part=None):
+        start, size = (0, chunk) if part is None else (part * half, half)
+        return picked.at[pl.ds(d * chunk + start, size)]
+
+    def part_copy(slot, target, relay, part=None):
+        rows = all_rows if part is None else pl.ds(part * half, half)
         return to_row(
-            picked.at[pl.ds(d * chunk, chunk)],
-            parts.at[my_row],
-            part_send.at[j],
-            part_recv.at[my_row],
-            d,
-        )
+            part_of(other(target), part),
+            parts.at[slot, rows],
+            part_send.at[slot],
+            part_recv.at[slot],
+            other(relay),
+        )
+
+    def part_copies():
+        return [
+            part_copy(0, 7, 1),
+            part_copy(1, 5, 7),
+            part_copy(2, 4, 6, 0),
+            part_copy(3, 1, 7),
+            part_copy(4, 3, 1),
+            part_copy(5, 4, 2, 1),
+        ]
+
+    def sum_copy(which, target):
+        slot = 6 + which
+        return to_row(
+            sums.at[which], parts.at[slot], part_send.at[slot], part_recv.at[slot], other(target)
+        )
+
+    def value_of(d):
+        return picked[pl.ds(pl.multiple_of(d * chunk, chunk), chunk), :]
 
     def top_copy(d):
         return to_row(
@@ -371,36 +417,25 @@
         s = other(j)
         to_row(table.at[s], table.at[s], send.at[j], recv.at[s], s).wait_recv()
 
-    two_stage = rows_dev == 8
-
     def hop(table, slot, part, d, send, recv):
         return to_row(table.at[slot, part], table.at[slot, part], send, recv, d)
 
     def stage_one(table, send, recv):
         return [
-            hop(table, my_row, pl.ds(0, chunk), other(j), send.at[j], recv.at[my_row])
-            for j in ((2, 6) if two_stage else range(1, rows_dev))
+            hop(table, my_row, all_rows, other(j), send.at[j], recv.at[my_row]) for j in (2, 6)
         ]
 
     def stage_two(table, send, recv):
-        if not two_stage:
-            return []
-        whole = pl.ds(0, chunk)
         below, above = other(6), other(2)
+        upper = pl.ds(0, half)
+        lower = pl.ds(half, half)
         return [
-            hop(table, below, whole, other(7), send.at[0], recv.at[below]),
-            hop(table, below, whole, other(1), send.at[1], recv.at[below]),
-            hop(table, below, pl.ds(0, chunk // 2), other(2), send.at[3], recv.at[below]),
-            hop(table, above, whole, other(1), send.at[4], recv.at[above]),
-            hop(table, above, whole, other(7), send.at[5], recv.at[above]),
-            hop(
-                table,
-                above,
-                pl.ds(chunk // 2, chunk // 2),
-                other(6),
-                send.at[7],
-                recv.at[rows_dev],
-            ),
+            hop(table, below, all_rows, other(7), send.at[0], recv.at[below]),
+            hop(table, below, all_rows, other(1), send.at[1], recv.at[below]),
+            hop(table, below, upper, other(2), send.at[3], recv.at[below]),
+            hop(table, above, all_rows, other(1), send.at[4], recv.at[above]),
+            hop(table, above, all_rows, other(7), send.at[5], recv.at[above]),
+            hop(table, above, lower, other(6), send.at[7], recv.at[rows_dev]),
         ]
 
     def begin(table, send, recv):
@@ -408,21 +443,15 @@
             copy.start()
 
     def forward(table, send, recv):
-        if two_stage:
-            arrive(6, table, send, recv)
-            arrive(2, table, send, recv)
+        arrive(6, table, send, recv)
+        arrive(2, table, send, recv)
         for copy in stage_two(table, send, recv):
             copy.start()
 
     def gathered(table, send, recv):
-        if not two_stage:
-            for j in range(1, rows_dev):
-                arrive(j, table, send, recv)
-            return
         for j in (1, 3, 5, 7):
             arrive(j, table, send, recv)
         far = other(4)
-        half = chunk // 2
         hop(table, far, pl.ds(0, half), far, send.at[0], recv.at[far]).wait_recv()
         hop(table, far, pl.ds(half, half), far, send.at[0], recv.at[rows_dev]).wait_recv()
 
@@ -452,9 +481,8 @@
         load.wait()
         pick(a_buf, picked)
 
-    for j in range(1, rows_dev):
-        part_copy(j).start()
-    parts[my_row] = picked[pl.ds(pl.multiple_of(my_row * chunk, chunk), chunk), :]
+    for copy in part_copies():
+        copy.start()
     for d in range(rows_dev):
         owner = d * chunk // NB
 
@@ -495,14 +523,21 @@
                 top_copy(d).wait_recv()
 
     begin(olds, old_send, old_recv)
-    for j in range(1, rows_dev):
-        arrive(j, parts, part_send, part_recv)
-    total = parts[0]
-    for s in range(1, rows_dev):
-        total = total + parts[s]
-    news[my_row] = total
+    for copy in part_copies():
+        copy.wait_recv()
+    low_sum = value_of(other(6)) + parts[0] + parts[1]
+    sums[0, :half] = low_sum[:half] + parts[2, :half]
+    sums[0, half:] = low_sum[half:]
+    high_sum = value_of(other(2)) + parts[3] + parts[4]
+    sums[1, :half] = high_sum[:half]
+    sums[1, half:] = high_sum[half:] + parts[5, half:]
+    sum_copy(0, 6).start()
+    sum_copy(1, 2).start()
+    forward(olds, old_send, old_recv)
+    sum_copy(0, 6).wait_recv()
+    sum_copy(1, 2).wait_recv()
+    news[my_row] = value_of(my_row) + parts[6] + parts[7]
     begin(news, new_send, new_recv)
-    forward(olds, old_send, old_recv)
 
     for c in range(2):
 
@@ -523,6 +558,16 @@
     groups = min(4, chips)
     per = chips // groups
 
+    def panel_copies(g):
+        size = per * slice_rows
+        copies = []
+        for side in range(2):
+            rows = pl.ds(side * half_rows + g * size, size)
+            copies.append(
+                pltpu.make_async_copy(panel.at[rows], panel_ref.at[rows], panel_out.at[2 * g + side])
+            )
+        return copies
+
     def pair_copy(g, which):
         held = pack.at[which, pl.ds(g * per, per)]
         return to_col(held, held, pair_send.at[g], pair_recv.at[g], chip * 2 + 1 - core)
@@ -546,23 +591,30 @@
             one_pack = pack[1, s]
             low = slice(slice_rows * s, slice_rows * (s + 1))
             high = slice(half_rows + slice_rows * s, half_rows + slice_rows * (s + 1))
-            panel_ref[low, :] = jnp.where(first, zero_pack, one_pack)
-            panel_ref[high, :] = pltpu.roll(jnp.where(first, one_pack, zero_pack), NB, 1)
-
+            panel[low, :] = jnp.where(first, zero_pack, one_pack)
+            panel[high, :] = pltpu.roll(jnp.where(first, one_pack, zero_pack), NB, 1)
+        for copy in panel_copies(g):
+            copy.start()
+
+    side = [
+        pltpu.make_async_copy(table, target, side_out.at[i])
+        for i, (table, target) in enumerate(
+            ((leads, leads_ref), (news, news_ref), (olds, olds_ref))
+        )
+    ]
     for j in range(1, rows_dev):
         arrive(j, leads, lead_send, lead_recv)
+    side[0].start()
+    gathered(olds, old_send, old_recv)
+    side[2].start()
     gathered(news, new_send, new_recv)
-    for d in range(rows_dev):
-        part = slice(chunk * d, chunk * (d + 1))
-        lead_ref[part, :] = leads[d, :chunk]
-        old_lead_ref[part, :] = leads[d, chunk:]
-        new_ref[part, :] = news[d]
-    gathered(olds, old_send, old_recv)
-    for d in range(rows_dev):
-        old_ref[chunk * d : chunk * (d + 1), :] = olds[d]
-
+    side[1].start()
+
+    for copy in part_copies():
+        copy.wait_send()
+    sum_copy(0, 6).wait_send()
+    sum_copy(1, 2).wait_send()
     for j in range(1, rows_dev):
-        part_copy(j).wait_send()
         ring_copy(j, leads, lead_send, lead_recv).wait_send()
     sent(news, new_send, new_recv)
     sent(olds, old_send, old_recv)
@@ -592,6 +644,10 @@
 
     for g in range(groups):
         pair_copy(g, core).wait_send()
+        for copy in panel_copies(g):
+            copy.wait()
+    for copy in side:
+        copy.wait()
 
 
 def move(matrix, pivots):
@@ -602,23 +658,21 @@
     rows, cols = matrix.shape
     dma = pltpu.SemaphoreType.DMA
     f32 = jnp.float32
-    vmem = pl.BlockSpec(memory_space=pltpu.VMEM)
     by_row = dma((rows_dev,))
     by_chip = dma((chips,))
     return pl.pallas_call(
         move_kernel,
         out_shape=[
             jax.ShapeDtypeStruct((rows, TOP), f32),
-            jax.ShapeDtypeStruct((TOP, cols), f32),
-            jax.ShapeDtypeStruct((TOP, cols), f32),
-            jax.ShapeDtypeStruct((TOP, TOP), f32),
-            jax.ShapeDtypeStruct((TOP, TOP), f32),
+            jax.ShapeDtypeStruct((rows_dev, 2 * chunk, TOP), f32),
+            jax.ShapeDtypeStruct((rows_dev, chunk, cols), f32),
+            jax.ShapeDtypeStruct((rows_dev, chunk, cols), f32),
         ],
         in_specs=[
             pl.BlockSpec(memory_space=pltpu.SMEM),
             pl.BlockSpec(memory_space=pl.ANY),
         ],
-        out_specs=[vmem] * 5,
+        out_specs=[pl.BlockSpec(memory_space=pl.ANY)] * 4,
         scratch_shapes=[
             pltpu.VMEM((rows, cols), f32),
             pltpu.VMEM((rows, TOP), f32),
@@ -632,6 +686,8 @@
             pltpu.VMEM((rows_dev, chunk, TOP), f32),
             pltpu.VMEM((2, chunk, TOP), f32),
             pltpu.VMEM((rows_dev, 2 * chunk, TOP), f32),
+            pltpu.VMEM((2, chunk, cols), f32),
+            pltpu.VMEM((rows, TOP), f32),
             dma((2,)),
             by_chip,
             by_chip,
@@ -652,6 +708,8 @@
             dma((2,)),
             by_row,
             by_row,
+            dma((8,)),
+            dma((3,)),
         ],
         compiler_params=pltpu.CompilerParams(collective_id=0, has_side_effects=True),
         name="move",
@@ -659,8 +717,8 @@
 
 
 def shards(matrix, pivots):
-    panel, new_top, old_top, lead, old_lead = move(matrix, pivots)
-    return finish(matrix, panel, lead, new_top, old_top, old_lead, pivots)
+    panel, leads, news, olds = move(matrix, pivots)
+    return finish(matrix, panel, leads, news, olds, pivots)
 
 
 def solution(mesh):

time: 47.2 us -> 49.3 us (1.044)
  the two profiles are of different devices: /device:TPU:32 before, /device:TPU:28 now
where the time goes in v1:
time: 49.3 us; the launch traced here: 49.2 us
  Pallas kernels  49.2 us (100%)
    pallas_call x1, Pallas kernels, move(): pl.pallas_call(move_kernel, out_shape=[jax.ShapeDtypeStruct((rows, TOP),...  37.4 us
    pallas_call x1, Pallas kernels, finish(): pl.pallas_call(finish_kernel, out_shape=jax.ShapeDtypeStruct(matrix.shape...  11.9 us

profile of v1, /device:TPU:28, one launch (start us, length us, event | category | flops | bytes accessed | tf_op | source)
XLA Modules:
  0.0 49.2 jit_solution(7426676114199006384)
XLA Ops:
  0.0 37.4 %move.1 = (f32[2048,128]{1,0:T(8,128)}, f32[8,32,128]{2,1,0:T(8,128)}, f32[8,16,512]{2,1,0:T(8,128)}, f32[8,16,512]{2,1,0:T(8,128)}) custom-call(s32[2,64]{1,0:T(2,128)} %pivot_ref.3, f32[2048,512]{1,0:T(8,128)} %a_ref.3), custom_call_target="tpu_custom_call" | custom-call | tf_op jit(solution)/shard_map/move/pallas_call | solution.py:663
  37.4 11.9 %finish.1 = f32[2048,512]{1,0:T(8,128)} custom-call(s32[2,64]{1,0:T(2,128)} %pivot_ref.3, f32[2048,512]{1,0:T(8,128)} %a_ref.3, f32[2048,128]{1,0:T(8,128)} %get-tuple-element.9.panel_ref, f32[8,32,128]{2,1,0:T(8,128)} %get-tuple-element.10.leads_ref, f32[8,16,512]{2,1,0:T(8,128)} %get-tuple-element.11.news_ref, f32[8,16,512]{2,1,0:T(8,128)} %get-tuple-element.12.olds_ref), custom_call_target="tpu_custom_call" | custom-call | tf_op jit(solution)/shard_map/finish/pallas_call | solution.py:209

commit v2 on v1

--- a/solution.py
+++ b/solution.py
@@ -50,59 +50,68 @@
 
 def factor(a_ref, lu_ref, linv_ref, uinv_ref):
     n = TOP // SUB
+    chunk = a_ref.shape[1] // 2
     lane = lax.broadcasted_iota(jnp.int32, (SUB, TOP), 1)
     sub = lax.broadcasted_iota(jnp.int32, (SUB, TOP), 0)
-    chunk = a_ref.shape[1] // 2
-    a = []
-    for i in range(n):
-        slot, start = divmod(SUB * i, chunk)
-        a.append(a_ref[slot, start : start + SUB, :])
-    low = [jnp.where(lane == sub + SUB * i, 1.0, 0.0).astype(jnp.float32) for i in range(n)]
-    upp = list(low)
+    row_id = lax.broadcasted_iota(jnp.int32, (TOP, TOP), 0)
+    lane_id = lax.broadcasted_iota(jnp.int32, (TOP, TOP), 1)
+    rest = jnp.concatenate([a_ref[slot, :chunk] for slot in range(TOP // chunk)], axis=0)
+    low_rest = jnp.where(row_id == lane_id, 1.0, 0.0).astype(jnp.float32)
+    eye = [low_rest[SUB * i : SUB * (i + 1)] for i in range(n)]
+    unit = [jnp.where(sub == j, 1.0, 0.0).astype(jnp.float32) for j in range(SUB)]
+    upp = None
     weights = jnp.ones((SUB, TOP), jnp.float32)
     for b in range(n):
         first = SUB * b
-        cols = [spread(a[b], first + j) for j in range(SUB)]
+        block, rest = rest[:SUB], rest[SUB:]
+        low, low_rest = low_rest[:SUB], low_rest[SUB:]
+        cols = [spread(block, first + j) for j in range(SUB)]
         weight, entry, a_line, low_line = [], [], [], []
         for k in range(SUB):
             weight.append(1.0 / line(cols[k], k))
             weights = jnp.where(lane == first + k, weight[k], weights)
             entry.append([line(cols[j], k) if j > k else None for j in range(SUB)])
-            a_line.append(jnp.where(lane > first + k, line(a[b], k), 0.0))
-            low_line.append(line(low[b], k))
+            a_line.append(jnp.where(lane > first + k, line(block, k), 0.0))
+            low_line.append(line(low, k))
             if k < SUB - 1:
                 multiplier = jnp.where(sub > k, cols[k] * weight[k], 0.0)
                 for j in range(k + 1, SUB):
                     cols[j] = cols[j] - multiplier * entry[k][j]
-                a[b] = a[b] - multiplier * a_line[k]
-                low[b] = low[b] - multiplier * low_line[k]
-
-        def multipliers(cols):
+                block = block - multiplier * a_line[k]
+                low = low - multiplier * low_line[k]
+        lu_ref[first : first + SUB, :] = block
+        linv_ref[first : first + SUB, :] = low
+
+        def over(x, rows):
+            return x[:1] if rows != SUB else x
+
+        def multipliers(cols, rows):
             cols = list(cols)
             for k in range(SUB):
-                cols[k] = cols[k] * weight[k]
+                cols[k] = cols[k] * over(weight[k], rows)
                 for j in range(k + 1, SUB):
-                    cols[j] = cols[j] - cols[k] * entry[k][j]
+                    cols[j] = cols[j] - cols[k] * over(entry[k][j], rows)
             return cols
 
-        for i in range(b + 1, n):
-            part = multipliers([spread(a[i], first + j) for j in range(SUB)])
+        rows = TOP - first - SUB
+        if rows:
+            part = multipliers([spread(rest, first + j) for j in range(SUB)], rows)
             for k in range(SUB):
-                a[i] = a[i] - part[k] * a_line[k]
-                low[i] = low[i] - part[k] * low_line[k]
-        for i in range(b + 1):
-            if i == b:
-                part = [jnp.where(sub == j, 1.0, 0.0).astype(jnp.float32) for j in range(SUB)]
-            else:
-                part = [spread(upp[i], first + j) for j in range(SUB)]
-            part = multipliers(part)
+                rest = rest - part[k] * over(a_line[k], rows)
+                low_rest = low_rest - part[k] * over(low_line[k], rows)
+        if upp is not None:
+            part = multipliers([spread(upp, first + j) for j in range(SUB)], first)
             for k in range(SUB):
-                upp[i] = upp[i] - part[k] * a_line[k]
-    for i in range(n):
-        part = slice(SUB * i, SUB * (i + 1))
-        lu_ref[part, :] = jnp.where(sub + SUB * i > lane, a[i] * weights, a[i])
-        linv_ref[part, :] = low[i]
-        uinv_ref[part, :] = upp[i] * weights
+                upp = upp - part[k] * over(a_line[k], first)
+        own = eye[b]
+        part = multipliers(unit, SUB)
+        for k in range(SUB):
+            own = own - part[k] * a_line[k]
+        upp = own if upp is None else jnp.concatenate([upp, own], axis=0)
+    scale = weights[:1]
+    packed = lu_ref[...]
+    lu_ref[...] = jnp.where(row_id > lane_id, packed * scale, packed)
+    uinv_ref[...] = upp * scale
 
 
 def finish_kernel(
@@ -112,14 +121,14 @@
     leads_ref,
     news_ref,
     olds_ref,
+    lu,
+    linv,
+    uinv,
     out_ref,
     a_buf,
     p_buf,
     news,
     olds,
-    lu,
-    linv,
-    uinv,
     upper,
     solved,
     top_rows,
@@ -143,7 +152,6 @@
         copy.start()
     for copy in copies:
         copy.start()
-    factor(leads_ref, lu, linv, uinv)
     news_copy.wait()
     upper[...] = dot(linv[...], news[...].reshape(upper.shape))
     solved[...] = dot(uinv[...], upper[...])
@@ -203,22 +211,20 @@
         out.wait()
 
 
-def finish(matrix, panel, leads, news, olds, pivots):
+def finish(matrix, panel, leads, news, olds, lu, linv, uinv, pivots):
     any_spec = pl.BlockSpec(memory_space=pl.ANY)
     vmem = pl.BlockSpec(memory_space=pltpu.VMEM)
     return pl.pallas_call(
         finish_kernel,
         out_shape=jax.ShapeDtypeStruct(matrix.shape, jnp.float32),
-        in_specs=[pl.BlockSpec(memory_space=pltpu.SMEM), any_spec, any_spec, vmem, any_spec, any_spec],
+        in_specs=[pl.BlockSpec(memory_space=pltpu.SMEM)]
+        + [any_spec, any_spec, vmem, any_spec, any_spec, vmem, vmem, vmem],
         out_specs=any_spec,
         scratch_shapes=[
             pltpu.VMEM(matrix.shape, jnp.float32),
             pltpu.VMEM(panel.shape, jnp.float32),
             pltpu.VMEM(news.shape, jnp.float32),
             pltpu.VMEM(olds.shape, jnp.float32),
-            pltpu.VMEM((TOP, TOP), jnp.float32),
-            pltpu.VMEM((TOP, TOP), jnp.float32),
-            pltpu.VMEM((TOP, TOP), jnp.float32),
             pltpu.VMEM((TOP, matrix.shape[1]), jnp.float32),
             pltpu.VMEM((TOP, matrix.shape[1]), jnp.float32),
             pltpu.VMEM((NB, matrix.shape[1]), jnp.float32),
@@ -227,7 +233,7 @@
             pltpu.SemaphoreType.DMA((CHUNKS,)),
         ],
         name="finish",
-    )(pivots, matrix, panel, leads, news, olds)
+    )(pivots, matrix, panel, leads, news, olds, lu, linv, uinv)
 
 
 def move_kernel(
@@ -237,6 +243,9 @@
     leads_ref,
     news_ref,
     olds_ref,
+    lu_ref,
+    linv_ref,
+    uinv_ref,
     a_buf,
     lead_buf,
     picked_lead,
@@ -584,6 +593,10 @@
 
         pair_copy(g, core).start()
 
+    for j in range(1, rows_dev):
+        arrive(j, leads, lead_send, lead_recv)
+    factor(leads, lu_ref, linv_ref, uinv_ref)
+
     for g in range(groups):
         pair_copy(g, 1 - core).wait_recv()
         for s in range(g * per, (g + 1) * per):
@@ -602,8 +615,6 @@
             ((leads, leads_ref), (news, news_ref), (olds, olds_ref))
         )
     ]
-    for j in range(1, rows_dev):
-        arrive(j, leads, lead_send, lead_recv)
     side[0].start()
     gathered(olds, old_send, old_recv)
     side[2].start()
@@ -667,12 +678,14 @@
             jax.ShapeDtypeStruct((rows_dev, 2 * chunk, TOP), f32),
             jax.ShapeDtypeStruct((rows_dev, chunk, cols), f32),
             jax.ShapeDtypeStruct((rows_dev, chunk, cols), f32),
+            *[jax.ShapeDtypeStruct((TOP, TOP), f32)] * 3,
         ],
         in_specs=[
             pl.BlockSpec(memory_space=pltpu.SMEM),
             pl.BlockSpec(memory_space=pl.ANY),
         ],
-        out_specs=[pl.BlockSpec(memory_space=pl.ANY)] * 4,
+        out_specs=[pl.BlockSpec(memory_space=pl.ANY)] * 4
+        + [pl.BlockSpec(memory_space=pltpu.VMEM)] * 3,
         scratch_shapes=[
             pltpu.VMEM((rows, cols), f32),
             pltpu.VMEM((rows, TOP), f32),
@@ -717,8 +730,8 @@
 
 
 def shards(matrix, pivots):
-    panel, leads, news, olds = move(matrix, pivots)
-    return finish(matrix, panel, leads, news, olds, pivots)
+    panel, leads, news, olds, lu, linv, uinv = move(matrix, pivots)
+    return finish(matrix, panel, leads, news, olds, lu, linv, uinv, pivots)
 
 
 def solution(mesh):

time: 49.3 us -> 48.1 us (0.976)
  Pallas kernels: 49.2 us -> 47.9 us
    pallas_call x1, Pallas kernels: 11.9 us -> 7.89 us  [finish(): pl.pallas_call(finish_kernel, out_shape=jax.ShapeDtypeStruct(matrix.shape...]
    pallas_call x1, Pallas kernels: 37.4 us -> 40 us  [move(): pl.pallas_call(move_kernel, out_shape=[jax.ShapeDtypeStruct((rows, TOP),...]
where the time goes in v2:
time: 48.1 us; the launch traced here: 47.9 us
  Pallas kernels  47.9 us (100%)
    pallas_call x1, Pallas kernels, move(): pl.pallas_call(move_kernel, out_shape=[jax.ShapeDtypeStruct((rows, TOP),...  40 us
    pallas_call x1, Pallas kernels, finish(): pl.pallas_call(finish_kernel, out_shape=jax.ShapeDtypeStruct(matrix.shape...  7.89 us

profile of v2, /device:TPU:28, one launch (start us, length us, event | category | flops | bytes accessed | tf_op | source)
XLA Modules:
  0.0 47.9 jit_solution(7490417179343663247)
XLA Ops:
  0.0 40.0 %move.1 = (f32[2048,128]{1,0:T(8,128)}, f32[8,32,128]{2,1,0:T(8,128)}, f32[8,16,512]{2,1,0:T(8,128)}, f32[8,16,512]{2,1,0:T(8,128)}, f32[128,128]{1,0:T(8,128)}, /*index=5*/f32[128,128]{1,0:T(8,128)}, f32[128,128]{1,0:T(8,128)}) custom-call(s32[2,64]{1,0:T(2,128)} %pivot_ref.3, f32[2048,512]{1,0:T(8,128)} %a_ref.3), custom_call_target="tpu_custom_call" | custom-call | tf_op jit(solution)/shard_map/move/pallas_call | solution.py:674
  40.0 7.9 %finish.1 = f32[2048,512]{1,0:T(8,128)} custom-call(s32[2,64]{1,0:T(2,128)} %pivot_ref.3, f32[2048,512]{1,0:T(8,128)} %a_ref.3, f32[2048,128]{1,0:T(8,128)} %get-tuple-element.12.panel_ref, f32[8,32,128]{2,1,0:T(8,128)} %get-tuple-element.13.leads_ref, f32[8,16,512]{2,1,0:T(8,128)} %get-tuple-element.14.news_ref, f32[8,16,512]{2,1,0:T(8,128)} %get-tuple-element.15.olds_ref, ...), custom_call_target="tpu_custom_call" | custom-call | tf_op jit(solution)/shard_map/finish/pallas_call | solution.py:217

commit v3 on v2

--- a/solution.py
+++ b/solution.py
@@ -138,7 +138,8 @@
 ):
     my_row = lax.axis_index("row")
     my_col = lax.axis_index("col")
-    rows = a_buf.shape[0] // CHUNKS
+    spare = a_buf.shape[0] - SUB
+    rows = spare // CHUNKS
     copies = [
         pltpu.make_async_copy(
             a_ref.at[pl.ds(rows * i, rows)], a_buf.at[pl.ds(rows * i, rows)], in_sem.at[i]
@@ -147,7 +148,7 @@
     ]
     news_copy = pltpu.make_async_copy(news_ref, news, side_sem.at[0])
     olds_copy = pltpu.make_async_copy(olds_ref, olds, side_sem.at[1])
-    panel_copy = pltpu.make_async_copy(panel_ref, p_buf, side_sem.at[2])
+    panel_copy = pltpu.make_async_copy(panel_ref, p_buf.at[pl.ds(0, spare)], side_sem.at[2])
     for copy in (news_copy, olds_copy, panel_copy):
         copy.start()
     for copy in copies:
@@ -173,23 +174,16 @@
         copy.wait()
 
     chunk = olds.shape[1]
-    bits = chunk.bit_length() - 1
-
-    def place(step, carry):
-        for j in range(PLACES):
-            k = step * PLACES + j
-            index = place_of(pivot_ref, k)
-
-            @pl.when(index >= 0)
-            def _():
-                slot = k >> bits
-                row = k & (chunk - 1)
-                a_buf[pl.ds(index, 1), :] = olds[slot, pl.ds(row, 1), :]
-                p_buf[pl.ds(index, 1), :] = leads_ref[slot, pl.ds(chunk + row, 1), :]
-
+
+    def place(slot, carry):
+        for row in range(chunk):
+            index = place_of(pivot_ref, slot * chunk + row)
+            index = jnp.where(index < 0, spare, index)
+            a_buf[pl.ds(index, 1), :] = olds[slot, row : row + 1, :]
+            p_buf[pl.ds(index, 1), :] = leads_ref[slot, chunk + row : chunk + row + 1, :]
         return carry
 
-    lax.fori_loop(0, TOP // PLACES, place, 0)
+    lax.fori_loop(0, TOP // chunk, place, 0)
     dropped = (lax.broadcasted_iota(jnp.int32, (rows, a_buf.shape[1]), 1) < NB) & holds
     outs = []
     for i in range(CHUNKS):
@@ -221,8 +215,8 @@
         + [any_spec, any_spec, vmem, any_spec, any_spec, vmem, vmem, vmem],
         out_specs=any_spec,
         scratch_shapes=[
-            pltpu.VMEM(matrix.shape, jnp.float32),
-            pltpu.VMEM(panel.shape, jnp.float32),
+            pltpu.VMEM((matrix.shape[0] + SUB, matrix.shape[1]), jnp.float32),
+            pltpu.VMEM((panel.shape[0] + SUB, TOP), jnp.float32),
             pltpu.VMEM(news.shape, jnp.float32),
             pltpu.VMEM(olds.shape, jnp.float32),
             pltpu.VMEM((TOP, matrix.shape[1]), jnp.float32),

time: 48.1 us -> 47.2 us (0.981)
  Pallas kernels: 47.9 us -> 47 us
    pallas_call x1, Pallas kernels: 7.89 us -> 7.03 us  [finish(): pl.pallas_call(finish_kernel, out_shape=jax.ShapeDtypeStruct(matrix.shape...]
where the time goes in v3:
time: 47.2 us; the launch traced here: 47 us
  Pallas kernels  47 us (100%)
    pallas_call x1, Pallas kernels, move(): pl.pallas_call(move_kernel, out_shape=[jax.ShapeDtypeStruct((rows, TOP),...  40 us
    pallas_call x1, Pallas kernels, finish(): pl.pallas_call(finish_kernel, out_shape=jax.ShapeDtypeStruct(matrix.shape...  7.03 us

profile of v3, /device:TPU:28, one launch (start us, length us, event | category | flops | bytes accessed | tf_op | source)
XLA Modules:
  0.0 47.0 jit_solution(11610685870233178722)
XLA Ops:
  0.0 40.0 %move.1 = (f32[2048,128]{1,0:T(8,128)}, f32[8,32,128]{2,1,0:T(8,128)}, f32[8,16,512]{2,1,0:T(8,128)}, f32[8,16,512]{2,1,0:T(8,128)}, f32[128,128]{1,0:T(8,128)}, /*index=5*/f32[128,128]{1,0:T(8,128)}, f32[128,128]{1,0:T(8,128)}) custom-call(s32[2,64]{1,0:T(2,128)} %pivot_ref.3, f32[2048,512]{1,0:T(8,128)} %a_ref.3), custom_call_target="tpu_custom_call" | custom-call | tf_op jit(solution)/shard_map/move/pallas_call | solution.py:668
  40.0 7.0 %finish.1 = f32[2048,512]{1,0:T(8,128)} custom-call(s32[2,64]{1,0:T(2,128)} %pivot_ref.3, f32[2048,512]{1,0:T(8,128)} %a_ref.3, f32[2048,128]{1,0:T(8,128)} %get-tuple-element.12.panel_ref, f32[8,32,128]{2,1,0:T(8,128)} %get-tuple-element.13.leads_ref, f32[8,16,512]{2,1,0:T(8,128)} %get-tuple-element.14.news_ref, f32[8,16,512]{2,1,0:T(8,128)} %get-tuple-element.15.olds_ref, ...), custom_call_target="tpu_custom_call" | custom-call | tf_op jit(solution)/shard_map/finish/pallas_call | solution.py:211

commit v4 on v3

--- a/solution.py
+++ b/solution.py
@@ -587,10 +587,6 @@
 
         pair_copy(g, core).start()
 
-    for j in range(1, rows_dev):
-        arrive(j, leads, lead_send, lead_recv)
-    factor(leads, lu_ref, linv_ref, uinv_ref)
-
     for g in range(groups):
         pair_copy(g, 1 - core).wait_recv()
         for s in range(g * per, (g + 1) * per):
@@ -602,6 +598,10 @@
             panel[high, :] = pltpu.roll(jnp.where(first, one_pack, zero_pack), NB, 1)
         for copy in panel_copies(g):
             copy.start()
+
+    for j in range(1, rows_dev):
+        arrive(j, leads, lead_send, lead_recv)
+    factor(leads, lu_ref, linv_ref, uinv_ref)
 
     side = [
         pltpu.make_async_copy(table, target, side_out.at[i])

time: 47.2 us -> 46.8 us (level)
  Pallas kernels: 47 us -> 46.5 us
    pallas_call x1, Pallas kernels: 40 us -> 39.4 us  [move(): pl.pallas_call(move_kernel, out_shape=[jax.ShapeDtypeStruct((rows, TOP),...]
where the time goes in v4:
time: 46.8 us; the launch traced here: 46.5 us
  Pallas kernels  46.5 us (99%)
    pallas_call x1, Pallas kernels, move(): pl.pallas_call(move_kernel, out_shape=[jax.ShapeDtypeStruct((rows, TOP),...  39.4 us
    pallas_call x1, Pallas kernels, finish(): pl.pallas_call(finish_kernel, out_shape=jax.ShapeDtypeStruct(matrix.shape...  7.03 us

profile of v4, /device:TPU:28, one launch (start us, length us, event | category | flops | bytes accessed | tf_op | source)
XLA Modules:
  0.0 46.5 jit_solution(10549453944745950158)
XLA Ops:
  0.0 39.4 %move.1 = (f32[2048,128]{1,0:T(8,128)}, f32[8,32,128]{2,1,0:T(8,128)}, f32[8,16,512]{2,1,0:T(8,128)}, f32[8,16,512]{2,1,0:T(8,128)}, f32[128,128]{1,0:T(8,128)}, /*index=5*/f32[128,128]{1,0:T(8,128)}, f32[128,128]{1,0:T(8,128)}) custom-call(s32[2,64]{1,0:T(2,128)} %pivot_ref.3, f32[2048,512]{1,0:T(8,128)} %a_ref.3), custom_call_target="tpu_custom_call" | custom-call | tf_op jit(solution)/shard_map/move/pallas_call | solution.py:668
  39.5 7.0 %finish.1 = f32[2048,512]{1,0:T(8,128)} custom-call(s32[2,64]{1,0:T(2,128)} %pivot_ref.3, f32[2048,512]{1,0:T(8,128)} %a_ref.3, f32[2048,128]{1,0:T(8,128)} %get-tuple-element.12.panel_ref, f32[8,32,128]{2,1,0:T(8,128)} %get-tuple-element.13.leads_ref, f32[8,16,512]{2,1,0:T(8,128)} %get-tuple-element.14.news_ref, f32[8,16,512]{2,1,0:T(8,128)} %get-tuple-element.15.olds_ref, ...), custom_call_target="tpu_custom_call" | custom-call | tf_op jit(solution)/shard_map/finish/pallas_call | solution.py:211
